TPU v7x, 512 devices: a whole 4x8x8 slice. The times are simulated.
512 devices in a mesh: rep: 64 (over x, y, core), tp: 8 (over z).
Axes of the slice: x: 4, y: 8, z: 8, core: 2. Of those that a mesh axis runs over, the one named last changes fastest.
Arguments:
- tokens: bfloat16 [16384, 8192], P('rep', 'tp'), may hold values from -6 to 6
- key_weight_base: bfloat16 [8192, 1024], P('tp'), may hold values from -0.0625 to 0.0625
- adapter_down_maps: bfloat16 [64, 8192, 64], P('rep', 'tp'), may hold values from -0.0625 to 0.0625
- adapter_up_maps: bfloat16 [64, 64, 1024], P('rep', None, 'tp'), may hold values from -0.75 to 0.75
- adapter_index: int32 [64, 256], P('rep'), may hold values from 0 to 63, never falling along the last dimension, each value on 1 to 8 neighbouring positions
- plan: int32 [16384, 1], P('rep'), may hold values from 0 to 63; in each aligned block of 256 rows (0 to 255, 256 to 511, ...) at most 8 rows name the same one
Outputs:
- keys_out: bfloat16 [32768, 1024], P('rep', 'tp')
Inputs may be any that keep to these rules, and one draw needn't show every extreme that they name: `adapter_index`: each replica's rows are ordered by adapter; at most 8 rows of one replica use one adapter, and some replica reaches it. `plan`: at most 8 rows of one replica have one destination, and some replica reaches it.
All inputs are finite; a program needn't handle non-finite values.
Results may differ from a plain program's by a relative error of at most 0.0045.
Values may be sent and summed in bfloat16 or wider, within the bound.
A program may use at most 64 MiB of HBM per device.

v0:
```python
import jax
import jax.numpy as jnp
from jax import lax
from jax.sharding import PartitionSpec as P


def per_device(tokens, key_weight_base, adapter_down_maps, adapter_up_maps, adapter_index, plan):
    rows = tokens.shape[0]
    key_feature_part = adapter_up_maps.shape[2]
    replica_count = lax.axis_size("rep")
    adapter_total = adapter_down_maps.shape[0] * replica_count
    seg_most = 2 * rows // adapter_total
    cap_move = 2 * rows // replica_count
    ids = adapter_index.reshape(rows)
    dest = plan.reshape(rows)
    base = lax.psum_scatter(
        lax.dot_general(
            key_weight_base, tokens, (((0,), (1,)), ((), ())), preferred_element_type=jnp.float32
        ),
        "tp",
        scatter_dimension=0,
        tiled=True,
    ).T
    adapter_range = jnp.arange(adapter_total, dtype=jnp.int32)
    slot_range = jnp.arange(seg_most, dtype=jnp.int32)
    starts = jnp.sum((ids[None, :] < adapter_range[:, None]).astype(jnp.int32), axis=1)
    counts = jnp.sum((ids[None, :] == adapter_range[:, None]).astype(jnp.int32), axis=1)
    index = jnp.clip(starts[:, None] + slot_range[None, :], 0, rows - 1)
    valid = slot_range[None, :] < counts[:, None]
    packed = jnp.where(valid[:, :, None], tokens[index], jnp.zeros((), tokens.dtype))
    block = packed
    upart = jnp.einsum(
        "asd,adr->asr",
        block,
        lax.all_gather(adapter_down_maps, "rep", axis=0, tiled=True),
        preferred_element_type=jnp.float32,
    )
    u_low = lax.psum(upart, "tp").astype(jnp.bfloat16)
    block = u_low
    delta = jnp.einsum(
        "asr,ark->ask",
        block,
        lax.all_gather(adapter_up_maps, "rep", axis=0, tiled=True),
        preferred_element_type=jnp.float32,
    )
    flat = ids * seg_most + jnp.arange(rows, dtype=jnp.int32) - starts[ids]
    row_delta = delta.reshape(adapter_total * seg_most, key_feature_part)[flat]
    keyrow = (base + 2.0 * row_delta).astype(jnp.bfloat16)
    dest_range = jnp.arange(replica_count, dtype=jnp.int32)
    onehot = (dest[:, None] == dest_range[None, :]).astype(jnp.int32)
    before = jnp.cumsum(onehot, axis=0, dtype=jnp.int32) - onehot
    slot = jnp.sum(before * onehot, axis=1)
    outgoing = (
        jnp.zeros((replica_count, cap_move, key_feature_part), jnp.bfloat16)
        .at[dest, slot]
        .set(keyrow)
    )
    arrived = lax.all_to_all(outgoing, "rep", split_axis=0, concat_axis=0, tiled=True)
    return arrived.reshape(replica_count * cap_move, key_feature_part)


def solution(mesh):
    placed = (
        P("rep", "tp"),
        P("tp", None),
        P("rep", "tp", None),
        P("rep", None, "tp"),
        P("rep", None),
        P("rep", None),
    )
    return jax.shard_map(
        per_device, mesh=mesh, in_specs=placed, out_specs=P("rep", "tp"), check_vma=False
    )
```

profile of v0, /device:TPU:1, one launch (start us, length us, event | category | flops | bytes accessed | tf_op | source)
XLA Modules:
  0.0 228.8 jit_solution(16918760003716140010)
XLA Ops:
  7.4 0.0 all-gather.3.cloned.1.call-start
  7.4 0.7 all-gather.3.cloned.1.call-update
  8.1 0.0 all-gather.5.cloned.1.call-start
  8.1 0.7 all-gather.5.cloned.1.call-update
  8.9 0.0 copy-start.3
  8.9 0.0 reduce-scatter.2.cloned.1.call-start
  8.9 0.0 copy-done
  9.0 2.8 %fusion.13 = f32[1024,256]{1,0:T(8,128)} fusion(bf16[1024,1024]{1,0:T(8,128)(2,1)S(1)} %copy-done, bf16[256,1024]{1,0:T(8,128)(2,1)} %param.6), kind=kOutput, calls=%fused_computation.42 | convolution fusion | flops 536870912 | bytes 3670016 | tf_op jit(solution)/shard_map/dot_general | solution.py:17
  11.7 0.0 reduce-scatter.2.cloned.1.call-update
  11.8 0.7 compare_select_fusion.2
  12.4 0.8 convert_reduce_fusion.1
  13.2 0.1 compare_select_fusion
  13.3 0.1 reshape.170
  13.5 2.8 %gather_fusion = bf16[512,1024]{1,0:T(8,128)(2,1)} fusion(bf16[256,1024]{1,0:T(8,128)(2,1)S(1)} %copy-done.1, s32[1024]{0:T(1024)S(1)} %pad_clamp_fusion.2), kind=kCustom, calls=%fused_computation | custom fusion | bytes 2099200 | tf_op jit(solution)/shard_map/gather | solution.py:30
  16.2 1.9 gather_fusion.1
  18.1 0.6 reduce-window.6
  18.8 0.2 slice_reduce_fusion
  19.0 0.1 fusion.7
  19.1 0.1 iota_compare_fusion.4
  19.2 86.5 %all-gather.3.cloned.1.call-done = bf16[64,1024,64]{1,2,0:T(8,128)(2,1)} async-done(((bf16[1,1024,64]{1,2,0:T(8,128)(2,1)}), bf16[64,1024,64]{1,2,0:T(8,128)(2,1)}) %all-gather.3.cloned.1.call-update) | async-done | bytes 8388624 | tf_op jit(solution)/shard_map/all_gather | solution.py:35
  105.7 6.0 %fusion = f32[64,8,64]{2,1,0:T(8,128)S(1)} fusion(bf16[64,1024,64]{1,2,0:T(8,128)(2,1)} %all-gather.3.cloned.1.call-done, bf16[512,1024]{1,0:T(8,128)(2,1)} %gather_fusion, pred[64,8]{1,0:T(8,128)(4,1)S(1)} %iota_compare_fusion.4), kind=kOutput, calls=%fused_computation.6 | convolution fusion | flops 67633152 | bytes 9568768 | tf_op jit(solution)/shard_map/asd,adr->asr/dot_general | solution.py:32
  111.8 27.4 %all-reduce.1 = bf16[64,8,64]{2,1,0:T(8,128)(2,1)S(1)} all-reduce(f32[64,8,64]{2,1,0:T(8,128)S(1)} %fusion), channel_id=1, replica_groups=mesh['rep'=64,'tp'=8] {'tp'}, use_global_device_ids=true, to_apply=%region_6.7 | all-reduce | flops 32768 | bytes 196608 | tf_op jit(solution)/shard_map/psum | solution.py:38
  139.2 49.1 %all-gather.5.cloned.1.call-done = bf16[64,64,128]{2,1,0:T(8,128)(2,1)} async-done(((bf16[1,64,128]{2,1,0:T(8,128)(2,1)}), bf16[64,64,128]{2,1,0:T(8,128)(2,1)}) %all-gather.5.cloned.1.call-update) | async-done | bytes 1048592 | tf_op jit(solution)/shard_map/all_gather | solution.py:43
  188.3 1.6 convolution_bitcast_fusion
  189.9 0.7 gather_fusion.2
  190.6 0.1 copy.16
  190.7 0.0 reduce-scatter.2.cloned.1.call-done
  190.8 0.9 fusion.3
  191.7 0.1 copy.17
  191.9 11.8 %scatter_fusion = bf16[64,8,128]{2,1,0:T(8,128)(2,1)S(1)} fusion(bf16[64,8,128]{2,1,0:T(8,128)(2,1)S(1)} %broadcast_in_dim.10, s32[256]{0:T(256)S(1)} %bitcast.53, bf16[256,128]{1,0:T(8,128)(2,1)S(1)} %copy.17), kind=kCustom, calls=%fused_computation.3 | custom fusion | bytes 198656 | tf_op jit(solution)/shard_map/scatter | solution.py:56
  203.7 17.0 %all_to_all.5 = bf16[64,8,128]{2,1,0:T(8,128)(2,1)S(1)} all-to-all(bf16[64,8,128]{2,1,0:T(8,128)(2,1)S(1)} %scatter_fusion), channel_id=1, replica_groups=mesh['rep'=64,'tp'=8] {'rep'}, dimensions={0} | all-to-all | bytes 262144 | tf_op jit(solution)/shard_map/all_to_all | solution.py:58
  220.7 0.7 copy.24
  (15 shorter events, 0.1 us)
Async XLA Ops:
  7.4 1.6 copy-start
  7.4 6.1 %copy-start.1 = (bf16[256,1024]{1,0:T(8,128)(2,1)S(1)}, bf16[256,1024]{1,0:T(8,128)(2,1)}, u32[]{:S(2)}) copy-start(bf16[256,1024]{1,0:T(8,128)(2,1)} %param.6) | copy-start | bytes 1572868
  7.4 98.4 %all-gather.3.cloned.1.call-start = ((), (), s32[]{:S(2)}) async-start(), calls=%async_computation.3 | async-start | bytes 8519680 | tf_op jit(solution)/shard_map/all_gather | solution.py:35
  8.1 180.2 %all-gather.5.cloned.1.call-start = ((), (), s32[]{:S(2)}) async-start(), calls=%async_computation.4 | async-start | bytes 1064960 | tf_op jit(solution)/shard_map/all_gather | solution.py:43
  8.8 9.3 %copy-start.2 = (s32[256,1]{0,1:T(1,128)S(1)}, s32[256,1]{0,1:T(1,128)}, u32[]{:S(2)}) copy-start(s32[256,1]{0,1:T(1,128)} %param.11) | copy-start | bytes 3076
  8.9 10.1 %copy-start.3 = (s32[1,256]{1,0:T(1,128)S(1)}, s32[1,256]{1,0:T(1,128)}, u32[]{:S(2)}) copy-start(s32[1,256]{1,0:T(1,128)} %param.10) | copy-start | bytes 3076
  8.9 181.9 %reduce-scatter.2.cloned.1.call-start = ((), (), s32[]{:S(2)}) async-start(), calls=%async_computation.2 | async-start | bytes 1179648 | tf_op jit(solution)/shard_map/reduce_scatter | solution.py:16
Sparse Core Ops, SparseCore 0:
  11.5 94.1 all-gather.2
  109.1 79.1 all-gather.4
Sparse Core Ops, SparseCore 1:
  12.2 43.7 reduce-scatter.1
where the time goes:
time: 229 us
  waiting for transfers between devices  137 us (60%)
  blocking collectives  44.4 us (19%)
  local copies, waits for them, and re-layouts  18.4 us (8%)
  between operations  15 us (7%)
  matrix products  10.4 us (5%)
  other arithmetic  3.37 us (1%)
    all_gather x1, waiting for transfers between devices, per_device(): lax.all_gather(adapter_down_maps, 'rep', axis=0, tiled=True)  86.5 us
    all_gather x1, waiting for transfers between devices, per_device(): lax.all_gather(adapter_up_maps, 'rep', axis=0, tiled=True)  49.1 us
    psum x1, blocking collectives, per_device(): u_low = lax.psum(upart, 'tp').astype(jnp.bfloat16)  27.4 us
    all_to_all x1, blocking collectives, per_device(): lax.all_to_all(outgoing, 'rep', split_axis=0, concat_axis=0, tiled=True)  17 us
    scatter x1, local copies, waits for them, and re-layouts, per_device(): outgoing = jnp.zeros((replica_count, cap_move, key_feature_part), jnp.bfl...  11.8 us
    dot_general x1, matrix products, per_device(): jnp.einsum('asd,adr->asr', block, lax.all_gather(adapter_down_maps, 'rep'...  6.04 us
  transfers between devices with their start and end apart: 3, of which 2 were waited for; matrix products, arithmetic and copies ran while one was open for 8% of the time, Pallas kernels for 0%

commit v1 on v0

v1 whole, which is shorter than its diff:
```python
import jax
import jax.numpy as jnp
from jax import lax
from jax.experimental import pallas as pl
from jax.experimental.pallas import tpu as pltpu
from jax.sharding import PartitionSpec as P

MESH = pl.DeviceIdType.MESH
F32 = jnp.float32
BF16 = jnp.bfloat16
NX, NY, NC, NZ = 4, 8, 2, 8
REP = NX * NY * NC
GRP = NX * NC
ROWS = 256
WIDTH = 1024
KEYS = 1024
RANK = 64
PART = 128
SLOTS = 8
PACK = REP * SLOTS


def iota(shape, dim):
    return lax.broadcasted_iota(jnp.int32, shape, dim)


def onehot(cond):
    return jnp.where(cond, 1.0, 0.0).astype(BF16)


def kernel(
    tok, w, down, up, ids, dest, out,
    psend, rrecv, dbuf, ubuf, bsend, brecv, csend, crecv, usend, urecv, dsend, drecv, osend, orecv, keyrow,
    s_x, r_x, s_yr, r_yr, s_yl, r_yl, s_ur, r_ur, s_ul, r_ul, s_b, r_b, s_c, r_c, s_u, r_u, s_d, r_d, s_o, r_o,
):
    me = lax.axis_index("rep")
    z = lax.axis_index("tp")
    mx = me // (NY * NC)
    my = (me // NC) % NY
    mc = me % NC
    mh = mx * NC + mc

    def rep_of(h, y):
        return ((h // NC) * NY + y) * NC + h % NC

    def grp(k):
        return (mh + k) % GRP

    def zp(k):
        return (z + k) % NZ

    barrier = pltpu.get_barrier_semaphore()

    def greet_rep(k, c):
        pl.semaphore_signal(barrier, inc=1, device_id={"rep": (me + k) % REP}, device_id_type=MESH)
        return c

    def greet_z(k, c):
        pl.semaphore_signal(barrier, inc=1, device_id={"tp": zp(k)}, device_id_type=MESH)
        return c

    lax.fori_loop(1, REP, greet_rep, 0)
    lax.fori_loop(1, NZ, greet_z, 0)

    eye = onehot(iota((RANK, RANK), 0) == iota((RANK, RANK), 1))
    dbuf[my] = lax.dot_general(eye, down[...], (((1,), (1,)), ((), ())), preferred_element_type=F32).astype(BF16)
    ubuf[my] = up[...]

    a = ids[...]
    lane = iota((1, ROWS), 1)
    rank = jnp.zeros((1, ROWS), jnp.int32)
    for k in range(1, SLOTS):
        rank = rank + jnp.where((lane >= k) & (pltpu.roll(a, k, 1) == a), 1, 0)
    ay = (a // NC) % NY
    spot = ((a // (NY * NC)) * NC + a % NC) * (NY * SLOTS) + (ay % 2) * 32 + (ay // 2) * SLOTS + rank
    pick = onehot(iota((PACK, ROWS), 0) == spot)
    for t in range(4):
        cols = slice(256 * t, 256 * t + 256)
        got = jnp.dot(pick, tok[:, cols], preferred_element_type=F32)
        psend[:, :, cols] = got.reshape(GRP, PACK // GRP, 256).astype(BF16)

    pl.semaphore_wait(barrier, REP - 1 + NZ - 1)

    right = rep_of(mh, (my + 1) % NY)
    left = rep_of(mh, (my + NY - 1) % NY)

    def ring(buf, ss, rs, s, to, step):
        i = (my + NY + step * s) % NY
        return pltpu.make_async_remote_copy(
            src_ref=buf.at[i], dst_ref=buf.at[i], send_sem=ss.at[s], recv_sem=rs.at[s],
            device_id={"rep": to}, device_id_type=MESH)

    to_right = [(ring(dbuf, s_yr, r_yr, s, right, -1), ring(ubuf, s_ur, r_ur, s, right, -1)) for s in range(4)]
    to_left = [(ring(dbuf, s_yl, r_yl, s, left, 1), ring(ubuf, s_ul, r_ul, s, left, 1)) for s in range(3)]
    for c in to_right[0] + to_left[0]:
        c.start()

    def xcopy(k):
        h = grp(k)
        return pltpu.make_async_remote_copy(
            src_ref=psend.at[h], dst_ref=rrecv.at[mh], send_sem=s_x.at[k], recv_sem=r_x.at[k],
            device_id={"rep": rep_of(h, my)}, device_id_type=MESH)

    def run(make, what, count):
        def body(k, c):
            getattr(make(k), what)()
            return c
        lax.fori_loop(1, count, body, 0)

    run(xcopy, "start", GRP)
    rrecv[mh] = psend[mh]

    for t in range(4):
        got = jnp.dot(tok[...], w[:, 256 * t:256 * t + 256], preferred_element_type=F32).astype(BF16)
        bsend[2 * t] = got[:, :PART]
        bsend[2 * t + 1] = got[:, PART:]

    def zcopy(src, dst, ss, rs):
        def make(k):
            return pltpu.make_async_remote_copy(
                src_ref=src(zp(k)), dst_ref=dst.at[z], send_sem=ss.at[k], recv_sem=rs.at[k],
                device_id={"tp": zp(k)}, device_id_type=MESH)
        return make

    bcopy = zcopy(lambda t: bsend.at[t], brecv, s_b, r_b)
    run(bcopy, "start", NZ)
    brecv[z] = bsend[z]

    square = iota((ROWS, ROWS), 0) == iota((ROWS, ROWS), 1)
    spot_col = jnp.sum(jnp.where(square, spot.astype(F32), 0.0), axis=1, keepdims=True).astype(jnp.int32)
    back = onehot(iota((ROWS, PACK), 1) == spot_col)
    d_col = dest[...]
    d_row = jnp.sum(jnp.where(square, d_col.astype(F32), 0.0), axis=0, keepdims=True).astype(jnp.int32)
    earlier = (d_col == d_row) & (iota((ROWS, ROWS), 0) < iota((ROWS, ROWS), 1))
    slot = jnp.sum(jnp.where(earlier, 1.0, 0.0), axis=0, keepdims=True).astype(jnp.int32)
    place = onehot(iota((PACK, ROWS), 0) == d_row * SLOTS + slot)

    for s in range(1, 4):
        for c in to_right[s - 1]:
            c.wait_recv()
        for c in to_right[s]:
            c.start()
        for c in to_left[s - 1]:
            c.wait_recv()
        if s < 3:
            for c in to_left[s]:
                c.start()
    for c in to_right[3]:
        c.wait_recv()
    run(xcopy, "wait_recv", GRP)

    r_all = rrecv[...].reshape(PACK, WIDTH)
    fold = jnp.zeros((PACK, PART), F32)
    row = iota((PACK, PART), 0)
    half = iota((PACK, PART), 1) // RANK
    mine = (row % 64) // 32 == half
    for t in range(2):
        d4 = dbuf[4 * t:4 * t + 4].reshape(4 * RANK, WIDTH)
        got = lax.dot_general(r_all, d4, (((1,), (1,)), ((), ())), preferred_element_type=F32)
        for i in range(2):
            keep = mine & ((row % 32) // SLOTS == 2 * t + i)
            fold = fold + jnp.where(keep, got[:, PART * i:PART * i + PART], 0.0)
    fold = fold.reshape(GRP, 2, 32, PART)
    csend[...] = fold[:, 0] + fold[:, 1]
    ccopy = zcopy(lambda t: csend.at[t], crecv, s_c, r_c)
    run(ccopy, "start", NZ)
    crecv[z] = csend[z]
    run(bcopy, "wait_recv", NZ)
    base = jnp.sum(brecv[...].astype(F32), axis=0)
    run(ccopy, "wait_recv", NZ)
    usend[...] = jnp.sum(crecv[...], axis=0).astype(BF16)
    ucopy = zcopy(lambda t: usend, urecv, s_u, r_u)
    run(ucopy, "start", NZ)
    urecv[z] = usend[...]
    run(ucopy, "wait_recv", NZ)

    u = urecv[...].reshape(PACK // 2, PART)
    row2 = iota((PACK // 2, PART), 0)
    half2 = iota((PACK // 2, PART), 1) // RANK
    u_all = ubuf[...].reshape(NY * RANK, PART)
    zero = jnp.zeros((), BF16)
    for p in range(2):
        wide = jnp.concatenate(
            [jnp.where(((row2 % 32) // SLOTS == i) & (half2 == p), u, zero) for i in range(4)], axis=1)
        got = jnp.dot(wide, u_all, preferred_element_type=F32)
        dsend[:, 32 * p:32 * p + 32] = got.reshape(GRP, 32, PART).astype(BF16)

    def dcopy(k):
        h = grp(k)
        return pltpu.make_async_remote_copy(
            src_ref=dsend.at[h], dst_ref=drecv.at[mh], send_sem=s_d.at[k], recv_sem=r_d.at[k],
            device_id={"rep": rep_of(h, my)}, device_id_type=MESH)

    run(dcopy, "start", GRP)
    drecv[mh] = dsend[mh]
    run(dcopy, "wait_recv", GRP)

    delta = jnp.dot(back, drecv[...].reshape(PACK, PART), preferred_element_type=F32)
    keyrow[...] = (base + 2.0 * delta).astype(BF16)
    got = jnp.dot(place, keyrow[...], preferred_element_type=F32)
    osend[...] = got.reshape(REP, SLOTS, PART).astype(BF16)

    def ocopy(k):
        to = (me + k) % REP
        return pltpu.make_async_remote_copy(
            src_ref=osend.at[to], dst_ref=orecv.at[me], send_sem=s_o.at[k], recv_sem=r_o.at[k],
            device_id={"rep": to}, device_id_type=MESH)

    run(ocopy, "start", REP)
    orecv[me] = osend[me]
    for pair in to_right + to_left:
        for c in pair:
            c.wait_send()
    run(xcopy, "wait_send", GRP)
    run(bcopy, "wait_send", NZ)
    run(ccopy, "wait_send", NZ)
    run(ucopy, "wait_send", NZ)
    run(dcopy, "wait_send", GRP)
    run(ocopy, "wait_recv", REP)
    run(ocopy, "wait_send", REP)
    out[...] = orecv[...]


def per_device(tokens, key_weight_base, adapter_down_maps, adapter_up_maps, adapter_index, plan):
    vm = pl.BlockSpec(memory_space=pltpu.VMEM)
    dma = pltpu.SemaphoreType.DMA
    got = pl.pallas_call(
        kernel,
        out_shape=jax.ShapeDtypeStruct((REP, SLOTS, PART), BF16),
        in_specs=[vm] * 6,
        out_specs=vm,
        scratch_shapes=[
            pltpu.VMEM((GRP, PACK // GRP, WIDTH), BF16),
            pltpu.VMEM((GRP, PACK // GRP, WIDTH), BF16),
            pltpu.VMEM((NY, RANK, WIDTH), BF16),
            pltpu.VMEM((NY, RANK, PART), BF16),
            pltpu.VMEM((NZ, ROWS, PART), BF16),
            pltpu.VMEM((NZ, ROWS, PART), BF16),
            pltpu.VMEM((GRP, 32, PART), F32),
            pltpu.VMEM((NZ, 32, PART), F32),
            pltpu.VMEM((32, PART), BF16),
            pltpu.VMEM((NZ, 32, PART), BF16),
            pltpu.VMEM((GRP, PACK // GRP, PART), BF16),
            pltpu.VMEM((GRP, PACK // GRP, PART), BF16),
            pltpu.VMEM((REP, SLOTS, PART), BF16),
            pltpu.VMEM((REP, SLOTS, PART), BF16),
            pltpu.VMEM((ROWS, PART), BF16),
            dma((GRP,)), dma((GRP,)),
            dma((4,)), dma((4,)), dma((3,)), dma((3,)),
            dma((4,)), dma((4,)), dma((3,)), dma((3,)),
            dma((NZ,)), dma((NZ,)),
            dma((NZ,)), dma((NZ,)),
            dma((NZ,)), dma((NZ,)),
            dma((GRP,)), dma((GRP,)),
            dma((REP,)), dma((REP,)),
        ],
        compiler_params=pltpu.CompilerParams(collective_id=0, has_side_effects=True),
        name="keys",
    )(
        tokens, key_weight_base, adapter_down_maps.reshape(WIDTH, RANK),
        adapter_up_maps.reshape(RANK, PART), adapter_index, plan,
    )
    return got.reshape(PACK, PART)


def solution(mesh):
    placed = (
        P("rep", "tp"),
        P("tp", None),
        P("rep", "tp", None),
        P("rep", None, "tp"),
        P("rep", None),
        P("rep", None),
    )
    return jax.shard_map(
        per_device, mesh=mesh, in_specs=placed, out_specs=P("rep", "tp"), check_vma=False
    )
```

time: 229 us -> 68.2 us (0.30)
  waiting for transfers between devices: 137 us -> 0 us
  Pallas kernels: 0 us -> 63.2 us
  blocking collectives: 44.4 us -> 0 us
  between operations: 15 us -> 0.01 us
  local copies, waits for them, and re-layouts: 18.4 us -> 4.77 us
  matrix products: 10.4 us -> 0 us
  other arithmetic: 3.37 us -> 0 us
    all_gather x2 -> x0, waiting for transfers between devices: 136 us -> none  [the longest x1 86.5 us: per_device(): lax.all_gather(adapter_down_maps, 'rep', axis=0, tiled=True)]
    pallas_call x0 -> x1, Pallas kernels: none -> 63.2 us  [per_device(): pl.pallas_call(kernel, out_shape=jax.ShapeDtypeStruct((REP, SLOTS, PART),...]
    psum x1 -> x0, blocking collectives: 27.4 us -> none  [per_device(): u_low = lax.psum(upart, 'tp').astype(jnp.bfloat16)]
    all_to_all x1 -> x0, blocking collectives: 17 us -> none  [per_device(): lax.all_to_all(outgoing, 'rep', split_axis=0, concat_axis=0, tiled=True)]
    scatter x1 -> x0, local copies, waits for them, and re-layouts: 11.8 us -> none  [per_device(): outgoing = jnp.zeros((replica_count, cap_move, key_feature_part), jnp.bfl...]
    dot_general x3 -> x0, matrix products: 10.4 us -> none  [the longest x1 6.04 us: per_device(): jnp.einsum('asd,adr->asr', block, lax.all_gather(adapter_down_maps, 'rep'...]
    gather x4 -> x0, local copies, waits for them, and re-layouts: 5.5 us -> none  [the longest x1 2.79 us: per_device(): tokens[index]]
    unnamed x9 -> x3, local copies, waits for them, and re-layouts: 0.71 us -> 4.77 us
  transfers between devices with their start and end apart: 3 -> 0, of which waited for: 2 -> 0; matrix products, arithmetic and copies ran while one was open for 8% -> 0% of each run, Pallas kernels for 0% -> 0%
where the time goes in v1:
time: 68.2 us; the launch traced here: 68 us
  Pallas kernels  63.2 us (93%)
  local copies, waits for them, and re-layouts  4.77 us (7%)
    pallas_call x1, Pallas kernels, per_device(): pl.pallas_call(kernel, out_shape=jax.ShapeDtypeStruct((REP, SLOTS, PART),...  63.2 us
    unnamed x3, local copies, waits for them, and re-layouts  4.77 us

profile of v1, /device:TPU:1, one launch (start us, length us, event | category | flops | bytes accessed | tf_op | source)
XLA Modules:
  0.0 68.0 jit_solution(12287090149856762444)
XLA Ops:
  0.0 1.5 %copy.8.dest = s32[256,1]{1,0:T(8,128)} copy(s32[256,1]{0,1:T(1,128)} %param.11) | data formatting | bytes 2048 | tf_op args[5]
  1.5 1.7 %copy.7 = bf16[1,1024,64]{2,1,0:T(8,128)(2,1)} copy(bf16[1,1024,64]{1,2,0:T(8,128)(2,1)} %param.8) | data formatting | bytes 262144 | tf_op args[2]
  3.2 63.2 %keys.1 = bf16[64,8,128]{2,1,0:T(8,128)(2,1)} custom-call(bf16[256,1024]{1,0:T(8,128)(2,1)} %tok.1, bf16[1024,1024]{1,0:T(8,128)(2,1)} %w.1, bf16[1024,64]{1,0:T(8,128)(2,1)} %bitcast.3, bf16[64,128]{1,0:T(8,128)(2,1)} %bitcast.5, s32[1,256]{1,0:T(1,128)} %ids.1, s32[256,1]{1,0:T(8,128)} %copy.8.dest), custom_call_target="tpu_custom_call" | custom-call | tf_op jit(solution)/shard_map/keys/pallas_call | solution.py:227
  66.4 1.6 %copy.10 = bf16[512,128]{1,0:T(8,128)(2,1)} copy(bf16[512,128]{1,0:T(8,128)(2,1)} %bitcast.4) | data formatting | bytes 262144

commit v2 on v1

v2 whole, which is shorter than its diff:
```python
import jax
import jax.numpy as jnp
from jax import lax
from jax.experimental import pallas as pl
from jax.experimental.pallas import tpu as pltpu
from jax.sharding import PartitionSpec as P

MESH = pl.DeviceIdType.MESH
F32 = jnp.float32
BF16 = jnp.bfloat16
NX, NY, NC, NZ = 4, 8, 2, 8
REP = NX * NY * NC
GRP = NX * NC
ROWS = 256
WIDTH = 1024
KEYS = 1024
RANK = 64
PART = 128
SLOTS = 8
PACK = REP * SLOTS


def iota(shape, dim):
    return lax.broadcasted_iota(jnp.int32, shape, dim)


def onehot(cond):
    return jnp.where(cond, 1.0, 0.0).astype(BF16)


def kernel(
    tok, w, down, up, ids, dest, out,
    wv, psend, rrecv, maps, bsend, brecv, csend, crecv, usend, urecv, dsend, drecv, osend, orecv,
    s_w, s_x, r_x, s_yr, r_yr, s_yl, r_yl, s_b, r_b, s_c, r_c, s_u, r_u, s_d, r_d, s_o, r_o,
):
    me = lax.axis_index("rep")
    z = lax.axis_index("tp")
    mx = me // (NY * NC)
    my = (me // NC) % NY
    mc = me % NC
    mh = mx * NC + mc

    def rep_of(h, y):
        return ((h // NC) * NY + y) * NC + h % NC

    def grp(k):
        return (mh + k) % GRP

    def zp(k):
        return (z + k) % NZ

    def rep_y(k):
        return rep_of(mh, (my + k) % NY)

    barrier = pltpu.get_barrier_semaphore()
    for k in (1, NY - 1):
        pl.semaphore_signal(barrier, inc=1, device_id={"rep": rep_y(k)}, device_id_type=MESH)
    for k in range(1, GRP):
        pl.semaphore_signal(barrier, inc=1, device_id={"rep": rep_of(grp(k), my)}, device_id_type=MESH)
    for k in range(1, NZ):
        pl.semaphore_signal(barrier, inc=1, device_id={"tp": zp(k)}, device_id_type=MESH)
    load_w = pltpu.make_async_copy(w, wv, s_w)
    load_w.start()

    maps[my, :, :, :WIDTH] = down[...].reshape(2, RANK // 2, WIDTH)
    maps[my, :, :, WIDTH:] = up[...].reshape(2, RANK // 2, PART)

    a = ids[...]
    lane = iota((1, ROWS), 1)
    rank = jnp.zeros((1, ROWS), jnp.int32)
    for k in range(1, SLOTS):
        rank = rank + jnp.where((lane >= k) & (pltpu.roll(a, k, 1) == a), 1, 0)
    ay = (a // NC) % NY
    spot = ((a // (NY * NC)) * NC + a % NC) * (NY * SLOTS) + (ay % 2) * 32 + (ay // 2) * SLOTS + rank
    pick = onehot(iota((PACK, ROWS), 0) == spot)
    for t in range(4):
        cols = slice(256 * t, 256 * t + 256)
        got = jnp.dot(pick, tok[:, cols], preferred_element_type=F32)
        psend[:, :, cols] = got.reshape(GRP, PACK // GRP, 256).astype(BF16)

    pl.semaphore_wait(barrier, 2 + GRP - 1 + NZ - 1)

    def ring(ss, rs, to, step, s, f):
        i = (my + NY + step * s) % NY
        return pltpu.make_async_remote_copy(
            src_ref=maps.at[i, f], dst_ref=maps.at[i, f], send_sem=ss.at[2 * s + f], recv_sem=rs.at[2 * s + f],
            device_id={"rep": to}, device_id_type=MESH)

    hops = [(s, f) for s in range(3) for f in range(2)]
    to_right = {h: ring(s_yr, r_yr, rep_y(1), -1, *h) for h in hops + [(3, 0)]}
    to_left = {h: ring(s_yl, r_yl, rep_y(NY - 1), 1, *h) for h in hops + [(3, 1)]}
    for f in range(2):
        to_right[0, f].start()
        to_left[0, f].start()

    def xcopy(k):
        h = grp(k)
        return pltpu.make_async_remote_copy(
            src_ref=psend.at[h], dst_ref=rrecv.at[mh], send_sem=s_x.at[k], recv_sem=r_x.at[k],
            device_id={"rep": rep_of(h, my)}, device_id_type=MESH)

    def run(make, what, count):
        def body(k, c):
            getattr(make(k), what)()
            return c
        lax.fori_loop(1, count, body, 0)

    run(xcopy, "start", GRP)
    rrecv[mh] = psend[mh]

    load_w.wait()
    for t in range(4):
        got = jnp.dot(tok[...], wv[:, 256 * t:256 * t + 256], preferred_element_type=F32).astype(BF16)
        bsend[2 * t] = got[:, :PART]
        bsend[2 * t + 1] = got[:, PART:]

    def zcopy(src, dst, ss, rs):
        def make(k):
            return pltpu.make_async_remote_copy(
                src_ref=src(zp(k)), dst_ref=dst.at[z], send_sem=ss.at[k], recv_sem=rs.at[k],
                device_id={"tp": zp(k)}, device_id_type=MESH)
        return make

    bcopy = zcopy(lambda t: bsend.at[t], brecv, s_b, r_b)
    run(bcopy, "start", NZ)
    brecv[z] = bsend[z]

    square = iota((ROWS, ROWS), 0) == iota((ROWS, ROWS), 1)
    spot_col = jnp.sum(jnp.where(square, spot.astype(F32), 0.0), axis=1, keepdims=True).astype(jnp.int32)
    back = onehot(iota((ROWS, PACK), 1) == spot_col)
    d_row = dest[...]
    d_col = jnp.sum(jnp.where(square, d_row.astype(F32), 0.0), axis=1, keepdims=True).astype(jnp.int32)
    earlier = (d_col == d_row) & (iota((ROWS, ROWS), 0) < iota((ROWS, ROWS), 1))
    slot = jnp.sum(jnp.where(earlier, 1.0, 0.0), axis=0, keepdims=True).astype(jnp.int32)
    place = onehot(iota((PACK, ROWS), 0) == d_row * SLOTS + slot)

    for s, f in hops:
        for way in (to_right, to_left):
            way[s, f].wait_recv()
            if (s + 1, f) in way:
                way[s + 1, f].start()
    to_right[3, 0].wait_recv()
    to_left[3, 1].wait_recv()
    run(xcopy, "wait_recv", GRP)

    r_all = rrecv[...].reshape(PACK, WIDTH)
    fold = jnp.zeros((PACK, PART), F32)
    row = iota((PACK, PART), 0)
    half = iota((PACK, PART), 1) // RANK
    mine = (row % 64) // 32 == half
    for t in range(2):
        d4 = maps[4 * t:4 * t + 4, :, :, :WIDTH].reshape(4 * RANK, WIDTH)
        got = lax.dot_general(r_all, d4, (((1,), (1,)), ((), ())), preferred_element_type=F32)
        for i in range(2):
            keep = mine & ((row % 32) // SLOTS == 2 * t + i)
            fold = fold + jnp.where(keep, got[:, PART * i:PART * i + PART], 0.0)
    fold = fold.reshape(GRP, 2, 32, PART)
    csend[...] = (fold[:, 0] + fold[:, 1]).astype(BF16)
    ccopy = zcopy(lambda t: csend.at[t], crecv, s_c, r_c)
    run(ccopy, "start", NZ)
    crecv[z] = csend[z]
    run(bcopy, "wait_recv", NZ)
    base = jnp.sum(brecv[...].astype(F32), axis=0)
    run(ccopy, "wait_recv", NZ)
    usend[...] = jnp.sum(crecv[...].astype(F32), axis=0).astype(BF16)
    ucopy = zcopy(lambda t: usend, urecv, s_u, r_u)
    run(ucopy, "start", NZ)
    urecv[z] = usend[...]
    run(ucopy, "wait_recv", NZ)

    u = urecv[...].astype(F32).reshape(NZ, 4, SLOTS, PART)
    first = iota((NZ * SLOTS, PART), 1) < RANK
    for i in range(4):
        ui = u[:, i].reshape(NZ * SLOTS, PART)
        both = jnp.concatenate([jnp.where(first, ui, 0.0), jnp.where(first, 0.0, ui)], axis=0).astype(BF16)
        up2 = maps[2 * i:2 * i + 2, :, :, WIDTH:].reshape(2 * RANK, PART)
        got = jnp.dot(both, up2, preferred_element_type=F32).astype(BF16)
        got = got.reshape(2, NZ, SLOTS, PART)
        for p in range(2):
            dsend[:, 32 * p + SLOTS * i:32 * p + SLOTS * i + SLOTS] = got[p]

    def dcopy(k):
        h = grp(k)
        return pltpu.make_async_remote_copy(
            src_ref=dsend.at[h], dst_ref=drecv.at[mh], send_sem=s_d.at[k], recv_sem=r_d.at[k],
            device_id={"rep": rep_of(h, my)}, device_id_type=MESH)

    run(dcopy, "start", GRP)
    drecv[mh] = dsend[mh]
    run(dcopy, "wait_recv", GRP)

    delta = jnp.dot(back, drecv[...].reshape(PACK, PART), preferred_element_type=F32)
    keyrow = (base + 2.0 * delta).astype(BF16)
    got = jnp.dot(place, keyrow, preferred_element_type=F32)
    osend[...] = got.reshape(REP, SLOTS, PART).astype(BF16)

    def ocopy(k):
        to = (me + k) % REP
        return pltpu.make_async_remote_copy(
            src_ref=osend.at[to], dst_ref=orecv.at[me], send_sem=s_o.at[k], recv_sem=r_o.at[k],
            device_id={"rep": to}, device_id_type=MESH)

    run(ocopy, "start", REP)
    orecv[me] = osend[me]
    for way in (to_right, to_left):
        for c in way.values():
            c.wait_send()
    run(xcopy, "wait_send", GRP)
    run(bcopy, "wait_send", NZ)
    run(ccopy, "wait_send", NZ)
    run(ucopy, "wait_send", NZ)
    run(dcopy, "wait_send", GRP)
    run(ocopy, "wait_recv", REP)
    run(ocopy, "wait_send", REP)
    out[...] = orecv[...]


def per_device(tokens, key_weight_base, adapter_down_maps, adapter_up_maps, adapter_index, plan):
    vm = pl.BlockSpec(memory_space=pltpu.VMEM)
    dma = pltpu.SemaphoreType.DMA
    got = pl.pallas_call(
        kernel,
        out_shape=jax.ShapeDtypeStruct((REP, SLOTS, PART), BF16),
        in_specs=[vm, pl.BlockSpec(memory_space=pl.ANY)] + [vm] * 4,
        out_specs=vm,
        scratch_shapes=[
            pltpu.VMEM((WIDTH, KEYS), BF16),
            pltpu.VMEM((GRP, PACK // GRP, WIDTH), BF16),
            pltpu.VMEM((GRP, PACK // GRP, WIDTH), BF16),
            pltpu.VMEM((NY, 2, RANK // 2, WIDTH + PART), BF16),
            pltpu.VMEM((NZ, ROWS, PART), BF16),
            pltpu.VMEM((NZ, ROWS, PART), BF16),
            pltpu.VMEM((GRP, 32, PART), BF16),
            pltpu.VMEM((NZ, 32, PART), BF16),
            pltpu.VMEM((32, PART), BF16),
            pltpu.VMEM((NZ, 32, PART), BF16),
            pltpu.VMEM((GRP, PACK // GRP, PART), BF16),
            pltpu.VMEM((GRP, PACK // GRP, PART), BF16),
            pltpu.VMEM((REP, SLOTS, PART), BF16),
            pltpu.VMEM((REP, SLOTS, PART), BF16),
            dma(()), dma((GRP,)), dma((GRP,)),
            dma((8,)), dma((8,)), dma((8,)), dma((8,)),
            dma((NZ,)), dma((NZ,)),
            dma((NZ,)), dma((NZ,)),
            dma((NZ,)), dma((NZ,)),
            dma((GRP,)), dma((GRP,)),
            dma((REP,)), dma((REP,)),
        ],
        compiler_params=pltpu.CompilerParams(collective_id=0, has_side_effects=True),
        name="keys",
    )(
        tokens, key_weight_base, adapter_down_maps.reshape(WIDTH, RANK).T,
        adapter_up_maps.reshape(RANK, PART), adapter_index, plan.reshape(1, ROWS),
    )
    return got.reshape(PACK, PART)


def solution(mesh):
    placed = (
        P("rep", "tp"),
        P("tp", None),
        P("rep", "tp", None),
        P("rep", None, "tp"),
        P("rep", None),
        P("rep", None),
    )
    return jax.shard_map(
        per_device, mesh=mesh, in_specs=placed, out_specs=P("rep", "tp"), check_vma=False
    )
```

time: 68.2 us -> 60.1 us (0.88)
  Pallas kernels: 63.2 us -> 58.4 us
  local copies, waits for them, and re-layouts: 4.77 us -> 1.57 us
    pallas_call x1, Pallas kernels: 63.2 us -> 58.4 us  [per_device(): pl.pallas_call(kernel, out_shape=jax.ShapeDtypeStruct((REP, SLOTS, PART),...]
    unnamed x3 -> x1, local copies, waits for them, and re-layouts: 4.77 us -> 1.57 us
where the time goes in v2:
time: 60.1 us; the launch traced here: 59.9 us
  Pallas kernels  58.4 us (97%)
  local copies, waits for them, and re-layouts  1.57 us (3%)
    pallas_call x1, Pallas kernels, per_device(): pl.pallas_call(kernel, out_shape=jax.ShapeDtypeStruct((REP, SLOTS, PART),...  58.4 us
    unnamed x1, local copies, waits for them, and re-layouts  1.57 us

profile of v2, /device:TPU:1, one launch (start us, length us, event | category | flops | bytes accessed | tf_op | source)
XLA Modules:
  0.0 59.9 jit_solution(16303284163258430216)
XLA Ops:
  0.0 58.4 %keys.1 = bf16[64,8,128]{2,1,0:T(8,128)(2,1)} custom-call(bf16[256,1024]{1,0:T(8,128)(2,1)} %tok.1, bf16[1024,1024]{1,0:T(8,128)(2,1)} %w.1, bf16[64,1024]{1,0:T(8,128)(2,1)} %bitcast.7, bf16[64,128]{1,0:T(8,128)(2,1)} %bitcast.8, s32[1,256]{1,0:T(1,128)} %ids.1, s32[1,256]{1,0:T(1,128)} %bitcast.9), custom_call_target="tpu_custom_call" | custom-call | tf_op jit(solution)/shard_map/keys/pallas_call | solution.py:221
  58.4 1.6 %copy.8 = bf16[512,128]{1,0:T(8,128)(2,1)} copy(bf16[512,128]{1,0:T(8,128)(2,1)} %bitcast.6) | data formatting | bytes 262144

commit v3 on v2

--- a/solution.py
+++ b/solution.py
@@ -18,6 +18,7 @@
 PART = 128
 SLOTS = 8
 PACK = REP * SLOTS
+PIECES = 4
 
 
 def iota(shape, dim):
@@ -43,11 +44,17 @@
     def rep_of(h, y):
         return ((h // NC) * NY + y) * NC + h % NC
 
-    def grp(k):
-        return (mh + k) % GRP
-
-    def zp(k):
-        return (z + k) % NZ
+    def far(n, ring):
+        return ring // 2 + (1 - 2 * (n % 2)) * ((n + 1) // 2)
+
+    def grp(n):
+        return ((mx + far(n // NC, NX)) % NX) * NC + (mc + 1 - n % NC) % NC
+
+    def zp(n):
+        return (z + far(n, NZ)) % NZ
+
+    def anyone(n):
+        return rep_of(grp(n % GRP), (my + far(n // GRP, NY)) % NY)
 
     def rep_y(k):
         return rep_of(mh, (my + k) % NY)
@@ -55,15 +62,15 @@
     barrier = pltpu.get_barrier_semaphore()
     for k in (1, NY - 1):
         pl.semaphore_signal(barrier, inc=1, device_id={"rep": rep_y(k)}, device_id_type=MESH)
-    for k in range(1, GRP):
+    for k in range(GRP - 1):
         pl.semaphore_signal(barrier, inc=1, device_id={"rep": rep_of(grp(k), my)}, device_id_type=MESH)
-    for k in range(1, NZ):
+    for k in range(NZ - 1):
         pl.semaphore_signal(barrier, inc=1, device_id={"tp": zp(k)}, device_id_type=MESH)
     load_w = pltpu.make_async_copy(w, wv, s_w)
     load_w.start()
 
-    maps[my, :, :, :WIDTH] = down[...].reshape(2, RANK // 2, WIDTH)
-    maps[my, :, :, WIDTH:] = up[...].reshape(2, RANK // 2, PART)
+    maps[my, :, :, :WIDTH] = down[...].reshape(PIECES, RANK // PIECES, WIDTH)
+    maps[my, :, :, WIDTH:] = up[...].reshape(PIECES, RANK // PIECES, PART)
 
     a = ids[...]
     lane = iota((1, ROWS), 1)
@@ -83,13 +90,15 @@
     def ring(ss, rs, to, step, s, f):
         i = (my + NY + step * s) % NY
         return pltpu.make_async_remote_copy(
-            src_ref=maps.at[i, f], dst_ref=maps.at[i, f], send_sem=ss.at[2 * s + f], recv_sem=rs.at[2 * s + f],
+            src_ref=maps.at[i, f], dst_ref=maps.at[i, f], send_sem=ss.at[PIECES * s + f], recv_sem=rs.at[PIECES * s + f],
             device_id={"rep": to}, device_id_type=MESH)
 
-    hops = [(s, f) for s in range(3) for f in range(2)]
-    to_right = {h: ring(s_yr, r_yr, rep_y(1), -1, *h) for h in hops + [(3, 0)]}
-    to_left = {h: ring(s_yl, r_yl, rep_y(NY - 1), 1, *h) for h in hops + [(3, 1)]}
-    for f in range(2):
+    hops = [(s, f) for s in range(3) for f in range(PIECES)]
+    last_right = [(3, f) for f in range(PIECES // 2)]
+    last_left = [(3, f) for f in range(PIECES // 2, PIECES)]
+    to_right = {h: ring(s_yr, r_yr, rep_y(1), -1, *h) for h in hops + last_right}
+    to_left = {h: ring(s_yl, r_yl, rep_y(NY - 1), 1, *h) for h in hops + last_left}
+    for f in range(PIECES):
         to_right[0, f].start()
         to_left[0, f].start()
 
@@ -103,7 +112,7 @@
         def body(k, c):
             getattr(make(k), what)()
             return c
-        lax.fori_loop(1, count, body, 0)
+        lax.fori_loop(0, count - 1, body, 0)
 
     run(xcopy, "start", GRP)
     rrecv[mh] = psend[mh]
@@ -139,8 +148,10 @@
             way[s, f].wait_recv()
             if (s + 1, f) in way:
                 way[s + 1, f].start()
-    to_right[3, 0].wait_recv()
-    to_left[3, 1].wait_recv()
+    for h in last_right:
+        to_right[h].wait_recv()
+    for h in last_left:
+        to_left[h].wait_recv()
     run(xcopy, "wait_recv", GRP)
 
     r_all = rrecv[...].reshape(PACK, WIDTH)
@@ -155,14 +166,14 @@
             keep = mine & ((row % 32) // SLOTS == 2 * t + i)
             fold = fold + jnp.where(keep, got[:, PART * i:PART * i + PART], 0.0)
     fold = fold.reshape(GRP, 2, 32, PART)
-    csend[...] = (fold[:, 0] + fold[:, 1]).astype(BF16)
+    csend[...] = fold[:, 0] + fold[:, 1]
     ccopy = zcopy(lambda t: csend.at[t], crecv, s_c, r_c)
     run(ccopy, "start", NZ)
     crecv[z] = csend[z]
     run(bcopy, "wait_recv", NZ)
     base = jnp.sum(brecv[...].astype(F32), axis=0)
     run(ccopy, "wait_recv", NZ)
-    usend[...] = jnp.sum(crecv[...].astype(F32), axis=0).astype(BF16)
+    usend[...] = jnp.sum(crecv[...], axis=0).astype(BF16)
     ucopy = zcopy(lambda t: usend, urecv, s_u, r_u)
     run(ucopy, "start", NZ)
     urecv[z] = usend[...]
@@ -195,7 +206,7 @@
     osend[...] = got.reshape(REP, SLOTS, PART).astype(BF16)
 
     def ocopy(k):
-        to = (me + k) % REP
+        to = anyone(k)
         return pltpu.make_async_remote_copy(
             src_ref=osend.at[to], dst_ref=orecv.at[me], send_sem=s_o.at[k], recv_sem=r_o.at[k],
             device_id={"rep": to}, device_id_type=MESH)
@@ -227,11 +238,11 @@
             pltpu.VMEM((WIDTH, KEYS), BF16),
             pltpu.VMEM((GRP, PACK // GRP, WIDTH), BF16),
             pltpu.VMEM((GRP, PACK // GRP, WIDTH), BF16),
-            pltpu.VMEM((NY, 2, RANK // 2, WIDTH + PART), BF16),
+            pltpu.VMEM((NY, PIECES, RANK // PIECES, WIDTH + PART), BF16),
             pltpu.VMEM((NZ, ROWS, PART), BF16),
             pltpu.VMEM((NZ, ROWS, PART), BF16),
-            pltpu.VMEM((GRP, 32, PART), BF16),
-            pltpu.VMEM((NZ, 32, PART), BF16),
+            pltpu.VMEM((GRP, 32, PART), F32),
+            pltpu.VMEM((NZ, 32, PART), F32),
             pltpu.VMEM((32, PART), BF16),
             pltpu.VMEM((NZ, 32, PART), BF16),
             pltpu.VMEM((GRP, PACK // GRP, PART), BF16),
@@ -239,7 +250,7 @@
             pltpu.VMEM((REP, SLOTS, PART), BF16),
             pltpu.VMEM((REP, SLOTS, PART), BF16),
             dma(()), dma((GRP,)), dma((GRP,)),
-            dma((8,)), dma((8,)), dma((8,)), dma((8,)),
+            dma((4 * PIECES,)), dma((4 * PIECES,)), dma((4 * PIECES,)), dma((4 * PIECES,)),
             dma((NZ,)), dma((NZ,)),
             dma((NZ,)), dma((NZ,)),
             dma((NZ,)), dma((NZ,)),

time: 60.1 us -> 59.3 us (0.987)
  Pallas kernels: 58.4 us -> 57.5 us
    pallas_call x1, Pallas kernels: 58.4 us -> 57.5 us  [per_device(): pl.pallas_call(kernel, out_shape=jax.ShapeDtypeStruct((REP, SLOTS, PART),...]
where the time goes in v3:
time: 59.3 us; the launch traced here: 59.1 us
  Pallas kernels  57.5 us (97%)
  local copies, waits for them, and re-layouts  1.57 us (3%)
    pallas_call x1, Pallas kernels, per_device(): pl.pallas_call(kernel, out_shape=jax.ShapeDtypeStruct((REP, SLOTS, PART),...  57.5 us
    unnamed x1, local copies, waits for them, and re-layouts  1.57 us

profile of v3, /device:TPU:1, one launch (start us, length us, event | category | flops | bytes accessed | tf_op | source)
XLA Modules:
  0.0 59.1 jit_solution(832129706334921428)
XLA Ops:
  0.0 57.5 %keys.1 = bf16[64,8,128]{2,1,0:T(8,128)(2,1)} custom-call(bf16[256,1024]{1,0:T(8,128)(2,1)} %tok.1, bf16[1024,1024]{1,0:T(8,128)(2,1)} %w.1, bf16[64,1024]{1,0:T(8,128)(2,1)} %bitcast.7, bf16[64,128]{1,0:T(8,128)(2,1)} %bitcast.8, s32[1,256]{1,0:T(1,128)} %ids.1, s32[1,256]{1,0:T(1,128)} %bitcast.9), custom_call_target="tpu_custom_call" | custom-call | tf_op jit(solution)/shard_map/keys/pallas_call | solution.py:232
  57.5 1.6 %copy.8 = bf16[512,128]{1,0:T(8,128)(2,1)} copy(bf16[512,128]{1,0:T(8,128)(2,1)} %bitcast.6) | data formatting | bytes 262144

commit v4 on v3

--- a/solution.py
+++ b/solution.py
@@ -30,9 +30,9 @@
 
 
 def kernel(
-    tok, w, down, up, ids, dest, out,
-    wv, psend, rrecv, maps, bsend, brecv, csend, crecv, usend, urecv, dsend, drecv, osend, orecv,
-    s_w, s_x, r_x, s_yr, r_yr, s_yl, r_yl, s_b, r_b, s_c, r_c, s_u, r_u, s_d, r_d, s_o, r_o,
+    tok_in, w_in, down_in, up_in, ids_in, dest_in, out,
+    tok, w, ids, dest, psend, rrecv, maps, ups, bsend, brecv, csend, crecv, usend, urecv, dsend, drecv, osend, orecv,
+    s_in, s_m, r_m, s_x, r_x, s_yr, r_yr, s_yl, r_yl, s_b, r_b, s_c, r_c, s_u, r_u, s_d, r_d, s_o, r_o,
 ):
     me = lax.axis_index("rep")
     z = lax.axis_index("tp")
@@ -66,11 +66,14 @@
         pl.semaphore_signal(barrier, inc=1, device_id={"rep": rep_of(grp(k), my)}, device_id_type=MESH)
     for k in range(NZ - 1):
         pl.semaphore_signal(barrier, inc=1, device_id={"tp": zp(k)}, device_id_type=MESH)
-    load_w = pltpu.make_async_copy(w, wv, s_w)
-    load_w.start()
-
-    maps[my, :, :, :WIDTH] = down[...].reshape(PIECES, RANK // PIECES, WIDTH)
-    maps[my, :, :, WIDTH:] = up[...].reshape(PIECES, RANK // PIECES, PART)
+
+    loads = [
+        pltpu.make_async_copy(src, dst, s_in.at[n]) for n, (src, dst) in enumerate((
+            (ids_in, ids), (dest_in, dest), (down_in, maps.at[my]), (tok_in, tok), (w_in, w), (up_in, ups.at[my])))
+    ]
+    for c in loads:
+        c.start()
+    loads[0].wait()
 
     a = ids[...]
     lane = iota((1, ROWS), 1)
@@ -80,11 +83,13 @@
     ay = (a // NC) % NY
     spot = ((a // (NY * NC)) * NC + a % NC) * (NY * SLOTS) + (ay % 2) * 32 + (ay // 2) * SLOTS + rank
     pick = onehot(iota((PACK, ROWS), 0) == spot)
+    loads[3].wait()
     for t in range(4):
         cols = slice(256 * t, 256 * t + 256)
         got = jnp.dot(pick, tok[:, cols], preferred_element_type=F32)
         psend[:, :, cols] = got.reshape(GRP, PACK // GRP, 256).astype(BF16)
 
+    loads[2].wait()
     pl.semaphore_wait(barrier, 2 + GRP - 1 + NZ - 1)
 
     def ring(ss, rs, to, step, s, f):
@@ -117,9 +122,9 @@
     run(xcopy, "start", GRP)
     rrecv[mh] = psend[mh]
 
-    load_w.wait()
+    loads[4].wait()
     for t in range(4):
-        got = jnp.dot(tok[...], wv[:, 256 * t:256 * t + 256], preferred_element_type=F32).astype(BF16)
+        got = jnp.dot(tok[...], w[:, 256 * t:256 * t + 256], preferred_element_type=F32).astype(BF16)
         bsend[2 * t] = got[:, :PART]
         bsend[2 * t + 1] = got[:, PART:]
 
@@ -137,6 +142,8 @@
     square = iota((ROWS, ROWS), 0) == iota((ROWS, ROWS), 1)
     spot_col = jnp.sum(jnp.where(square, spot.astype(F32), 0.0), axis=1, keepdims=True).astype(jnp.int32)
     back = onehot(iota((ROWS, PACK), 1) == spot_col)
+    loads[1].wait()
+    loads[5].wait()
     d_row = dest[...]
     d_col = jnp.sum(jnp.where(square, d_row.astype(F32), 0.0), axis=1, keepdims=True).astype(jnp.int32)
     earlier = (d_col == d_row) & (iota((ROWS, ROWS), 0) < iota((ROWS, ROWS), 1))
@@ -152,6 +159,13 @@
         to_right[h].wait_recv()
     for h in last_left:
         to_left[h].wait_recv()
+
+    def mcopy(k):
+        return pltpu.make_async_remote_copy(
+            src_ref=ups.at[my], dst_ref=ups.at[my], send_sem=s_m.at[k], recv_sem=r_m.at[k],
+            device_id={"rep": rep_y(far(k, NY))}, device_id_type=MESH)
+
+    run(mcopy, "start", NY)
     run(xcopy, "wait_recv", GRP)
 
     r_all = rrecv[...].reshape(PACK, WIDTH)
@@ -160,7 +174,7 @@
     half = iota((PACK, PART), 1) // RANK
     mine = (row % 64) // 32 == half
     for t in range(2):
-        d4 = maps[4 * t:4 * t + 4, :, :, :WIDTH].reshape(4 * RANK, WIDTH)
+        d4 = maps[4 * t:4 * t + 4].reshape(4 * RANK, WIDTH)
         got = lax.dot_general(r_all, d4, (((1,), (1,)), ((), ())), preferred_element_type=F32)
         for i in range(2):
             keep = mine & ((row % 32) // SLOTS == 2 * t + i)
@@ -179,12 +193,13 @@
     urecv[z] = usend[...]
     run(ucopy, "wait_recv", NZ)
 
+    run(mcopy, "wait_recv", NY)
     u = urecv[...].astype(F32).reshape(NZ, 4, SLOTS, PART)
     first = iota((NZ * SLOTS, PART), 1) < RANK
     for i in range(4):
         ui = u[:, i].reshape(NZ * SLOTS, PART)
         both = jnp.concatenate([jnp.where(first, ui, 0.0), jnp.where(first, 0.0, ui)], axis=0).astype(BF16)
-        up2 = maps[2 * i:2 * i + 2, :, :, WIDTH:].reshape(2 * RANK, PART)
+        up2 = ups[2 * i:2 * i + 2].reshape(2 * RANK, PART)
         got = jnp.dot(both, up2, preferred_element_type=F32).astype(BF16)
         got = got.reshape(2, NZ, SLOTS, PART)
         for p in range(2):
@@ -216,6 +231,7 @@
     for way in (to_right, to_left):
         for c in way.values():
             c.wait_send()
+    run(mcopy, "wait_send", NY)
     run(xcopy, "wait_send", GRP)
     run(bcopy, "wait_send", NZ)
     run(ccopy, "wait_send", NZ)
@@ -232,13 +248,17 @@
     got = pl.pallas_call(
         kernel,
         out_shape=jax.ShapeDtypeStruct((REP, SLOTS, PART), BF16),
-        in_specs=[vm, pl.BlockSpec(memory_space=pl.ANY)] + [vm] * 4,
+        in_specs=[pl.BlockSpec(memory_space=pl.ANY)] * 6,
         out_specs=vm,
         scratch_shapes=[
+            pltpu.VMEM((ROWS, WIDTH), BF16),
             pltpu.VMEM((WIDTH, KEYS), BF16),
+            pltpu.VMEM((1, ROWS), jnp.int32),
+            pltpu.VMEM((1, ROWS), jnp.int32),
             pltpu.VMEM((GRP, PACK // GRP, WIDTH), BF16),
             pltpu.VMEM((GRP, PACK // GRP, WIDTH), BF16),
-            pltpu.VMEM((NY, PIECES, RANK // PIECES, WIDTH + PART), BF16),
+            pltpu.VMEM((NY, PIECES, RANK // PIECES, WIDTH), BF16),
+            pltpu.VMEM((NY, RANK, PART), BF16),
             pltpu.VMEM((NZ, ROWS, PART), BF16),
             pltpu.VMEM((NZ, ROWS, PART), BF16),
             pltpu.VMEM((GRP, 32, PART), F32),
@@ -249,7 +269,7 @@
             pltpu.VMEM((GRP, PACK // GRP, PART), BF16),
             pltpu.VMEM((REP, SLOTS, PART), BF16),
             pltpu.VMEM((REP, SLOTS, PART), BF16),
-            dma(()), dma((GRP,)), dma((GRP,)),
+            dma((6,)), dma((NY,)), dma((NY,)), dma((GRP,)), dma((GRP,)),
             dma((4 * PIECES,)), dma((4 * PIECES,)), dma((4 * PIECES,)), dma((4 * PIECES,)),
             dma((NZ,)), dma((NZ,)),
             dma((NZ,)), dma((NZ,)),
@@ -260,7 +280,7 @@
         compiler_params=pltpu.CompilerParams(collective_id=0, has_side_effects=True),
         name="keys",
     )(
-        tokens, key_weight_base, adapter_down_maps.reshape(WIDTH, RANK).T,
+        tokens, key_weight_base, adapter_down_maps.reshape(WIDTH, RANK).T.reshape(PIECES, RANK // PIECES, WIDTH),
         adapter_up_maps.reshape(RANK, PART), adapter_index, plan.reshape(1, ROWS),
     )
     return got.reshape(PACK, PART)

time: 59.3 us -> 58.4 us (0.985)
  Pallas kernels: 57.5 us -> 56.7 us
    pallas_call x1, Pallas kernels: 57.5 us -> 56.7 us  [per_device(): pl.pallas_call(kernel, out_shape=jax.ShapeDtypeStruct((REP, SLOTS, PART),...]
where the time goes in v4:
time: 58.4 us; the launch traced here: 58.2 us
  Pallas kernels  56.7 us (97%)
  local copies, waits for them, and re-layouts  1.57 us (3%)
    pallas_call x1, Pallas kernels, per_device(): pl.pallas_call(kernel, out_shape=jax.ShapeDtypeStruct((REP, SLOTS, PART),...  56.7 us
    unnamed x1, local copies, waits for them, and re-layouts  1.57 us

profile of v4, /device:TPU:1, one launch (start us, length us, event | category | flops | bytes accessed | tf_op | source)
XLA Modules:
  0.0 58.2 jit_solution(14242860538283238540)
XLA Ops:
  0.0 56.7 %keys.1 = bf16[64,8,128]{2,1,0:T(8,128)(2,1)} custom-call(bf16[256,1024]{1,0:T(8,128)(2,1)} %tok_in.1, bf16[1024,1024]{1,0:T(8,128)(2,1)} %w_in.1, bf16[4,16,1024]{2,1,0:T(8,128)(2,1)} %bitcast.9, bf16[64,128]{1,0:T(8,128)(2,1)} %bitcast.10, s32[1,256]{1,0:T(1,128)} %ids_in.1, s32[1,256]{1,0:T(1,128)} %bitcast.11), custom_call_target="tpu_custom_call" | custom-call | tf_op jit(solution)/shard_map/keys/pallas_call | solution.py:248
  56.7 1.6 %copy.8 = bf16[512,128]{1,0:T(8,128)(2,1)} copy(bf16[512,128]{1,0:T(8,128)(2,1)} %bitcast.8) | data formatting | bytes 262144

commit v5 on v4

--- a/solution.py
+++ b/solution.py
@@ -139,17 +139,7 @@
     run(bcopy, "start", NZ)
     brecv[z] = bsend[z]
 
-    square = iota((ROWS, ROWS), 0) == iota((ROWS, ROWS), 1)
-    spot_col = jnp.sum(jnp.where(square, spot.astype(F32), 0.0), axis=1, keepdims=True).astype(jnp.int32)
-    back = onehot(iota((ROWS, PACK), 1) == spot_col)
-    loads[1].wait()
     loads[5].wait()
-    d_row = dest[...]
-    d_col = jnp.sum(jnp.where(square, d_row.astype(F32), 0.0), axis=1, keepdims=True).astype(jnp.int32)
-    earlier = (d_col == d_row) & (iota((ROWS, ROWS), 0) < iota((ROWS, ROWS), 1))
-    slot = jnp.sum(jnp.where(earlier, 1.0, 0.0), axis=0, keepdims=True).astype(jnp.int32)
-    place = onehot(iota((PACK, ROWS), 0) == d_row * SLOTS + slot)
-
     for s, f in hops:
         for way in (to_right, to_left):
             way[s, f].wait_recv()
@@ -184,6 +174,17 @@
     ccopy = zcopy(lambda t: csend.at[t], crecv, s_c, r_c)
     run(ccopy, "start", NZ)
     crecv[z] = csend[z]
+
+    square = iota((ROWS, ROWS), 0) == iota((ROWS, ROWS), 1)
+    spot_col = jnp.sum(jnp.where(square, spot.astype(F32), 0.0), axis=1, keepdims=True).astype(jnp.int32)
+    back = onehot(iota((ROWS, PACK), 1) == spot_col)
+    loads[1].wait()
+    d_row = dest[...]
+    d_col = jnp.sum(jnp.where(square, d_row.astype(F32), 0.0), axis=1, keepdims=True).astype(jnp.int32)
+    earlier = (d_col == d_row) & (iota((ROWS, ROWS), 0) < iota((ROWS, ROWS), 1))
+    slot = jnp.sum(jnp.where(earlier, 1.0, 0.0), axis=0, keepdims=True).astype(jnp.int32)
+    place = onehot(iota((PACK, ROWS), 0) == d_row * SLOTS + slot)
+
     run(bcopy, "wait_recv", NZ)
     base = jnp.sum(brecv[...].astype(F32), axis=0)
     run(ccopy, "wait_recv", NZ)

time: 58.4 us -> 58.4 us (level)
  no operation moved by 1% of the time
where the time goes in v5:
time: 58.4 us; the launch traced here: 58.2 us
  Pallas kernels  56.7 us (97%)
  local copies, waits for them, and re-layouts  1.57 us (3%)
    pallas_call x1, Pallas kernels, per_device(): pl.pallas_call(kernel, out_shape=jax.ShapeDtypeStruct((REP, SLOTS, PART),...  56.7 us
    unnamed x1, local copies, waits for them, and re-layouts  1.57 us

profile of v5, /device:TPU:1, one launch (start us, length us, event | category | flops | bytes accessed | tf_op | source)
XLA Modules:
  0.0 58.2 jit_solution(5579999543064479646)
XLA Ops:
  0.0 56.7 %keys.1 = bf16[64,8,128]{2,1,0:T(8,128)(2,1)} custom-call(bf16[256,1024]{1,0:T(8,128)(2,1)} %tok_in.1, bf16[1024,1024]{1,0:T(8,128)(2,1)} %w_in.1, bf16[4,16,1024]{2,1,0:T(8,128)(2,1)} %bitcast.9, bf16[64,128]{1,0:T(8,128)(2,1)} %bitcast.10, s32[1,256]{1,0:T(1,128)} %ids_in.1, s32[1,256]{1,0:T(1,128)} %bitcast.11), custom_call_target="tpu_custom_call" | custom-call | tf_op jit(solution)/shard_map/keys/pallas_call | solution.py:249
  56.7 1.6 %copy.8 = bf16[512,128]{1,0:T(8,128)(2,1)} copy(bf16[512,128]{1,0:T(8,128)(2,1)} %bitcast.8) | data formatting | bytes 262144
